TPU v7x, 512 devices: a whole 4x4x16 slice. The times are simulated.
512 devices in a mesh: tm: 64 (over z, y), tensor: 8 (over x, core).
Axes of the slice: x: 4, y: 4, z: 16, core: 2. Of those that a mesh axis runs over, the one named last changes fastest.
Arguments:
- query_input: bfloat16 [24576, 2048], P('tm', 'tensor'), may hold values from -6 to 6
- key_input: bfloat16 [24576, 2048], P('tm', 'tensor'), may hold values from -6 to 6
- value_input: bfloat16 [24576, 2048], P('tm', 'tensor'), may hold values from -6 to 6
- log_decay: float32 [16, 24576], P('tensor', 'tm'), may hold values from -0.75 to 0, as said below
- stretch_ids: int32 [24576], P('tm'), may hold values from 0 to 383, as said below
- norm_gain: float32 [2048], P('tensor'), may hold values from 0.1 to 1.9
- out_weight: bfloat16 [2048, 4096], P('tensor'), may hold values from -0.125 to 0.125
- out_cotangent: bfloat16 [24576, 4096], P(('tm', 'tensor')), may hold values from -6 to 6
Outputs:
- layer_out: bfloat16 [24576, 4096], P(('tm', 'tensor'))
- query_grad: bfloat16 [24576, 2048], P('tm', 'tensor')
- key_grad: bfloat16 [24576, 2048], P('tm', 'tensor')
- value_grad: bfloat16 [24576, 2048], P('tm', 'tensor')
Inputs may be any that keep to these rules, and one draw needn't show every extreme that they name: `stretch_ids`: stretch ids never fall along the tokens, start at 0 and rise by at most one at a time, change only at multiples of 32 tokens, and rise at every multiple of 384 tokens, so that no stretch crosses a block; every block holds exactly 6 stretches. `log_decay`: every entry is negative.
All inputs are finite; a program needn't handle non-finite values.
Results may differ from a plain program's by a relative error of at most 0.014.
Values may be sent and summed in bfloat16 or wider, within the bound.
No kernel may reach another device: no remote copies, remote signals or barrier semaphores. Data moves between devices by JAX's collectives and lax.ppermute only.
A program may use at most 64 MiB of HBM per device.

v0:
```python
import jax
import jax.numpy as jnp
from jax import lax
from jax.sharding import PartitionSpec as P

EPSILON = 1e-06


def entering(part, axis, combine, identity):
    count = lax.axis_size(axis)
    place = lax.axis_index(axis)
    ahead = count - 1 - place
    gathered = jax.tree.map(lambda a: lax.all_gather(a, axis), part)
    state = jax.tree.map(lambda a, e: jnp.zeros_like(a) + jnp.asarray(e, a.dtype), part, identity)

    def one(turn, state):
        source = count - 1 - turn
        return combine(
            state, jax.tree.map(lambda a: lax.dynamic_index_in_dim(a, source, 0, False), gathered)
        )

    return lax.fori_loop(0, ahead, one, state)


def chain_combine(earlier, later):
    return (earlier[0] * later[0], later[0][:, None, None] * earlier[1] + later[1])


def on_device(
    query_input,
    key_input,
    value_input,
    log_decay,
    stretch_ids,
    norm_gain,
    out_weight,
    out_cotangent,
):
    highest = lax.Precision.HIGHEST
    tok_rows = query_input.shape[0]
    heads = log_decay.shape[0]
    head_size = query_input.shape[1] // heads
    query_pos = jnp.maximum(query_input, 0).reshape(tok_rows, heads, head_size)
    key_pos = jnp.maximum(key_input, 0).reshape(tok_rows, heads, head_size)
    value_act = value_input.reshape(tok_rows, heads, head_size)
    cumulative = jnp.cumsum(log_decay, axis=1)
    same_stretch = stretch_ids[:, None] == stretch_ids[None, :]
    visible = stretch_ids[None, :] <= stretch_ids[:, None]
    stretch_end = jnp.min(jnp.where(same_stretch[None], cumulative[:, None, :], jnp.inf), axis=2)
    block_end = cumulative[:, -1]
    weights = jnp.where(
        visible[None],
        jnp.exp(jnp.minimum(stretch_end[:, :, None] - cumulative[:, None, :], 0.0)),
        0.0,
    )
    scores = jnp.einsum("iha,jha->hij", query_pos, key_pos, preferred_element_type=jnp.float32)
    probs = (weights * scores).astype(jnp.bfloat16)
    local_out = jnp.einsum("hij,jhb->ihb", probs, value_act, preferred_element_type=jnp.float32)
    key_scale = jnp.exp(block_end[:, None] - cumulative).T
    decayed = (key_scale[:, :, None] * key_pos).astype(jnp.bfloat16)
    block_state = jnp.einsum("jha,jhb->hab", decayed, value_act, preferred_element_type=jnp.float32)
    block_decay = jnp.exp(block_end)
    identity = (jnp.ones_like(block_decay), jnp.zeros_like(block_state))
    totals = lax.all_gather(block_end[None, :], "tm", axis=0, tiled=True)
    running = jnp.cumsum(totals, axis=0)
    here = lax.axis_index("tm")
    before_here = lax.dynamic_index_in_dim(running, jnp.maximum(here - 1, 0), 0, keepdims=False)
    order = jnp.arange(totals.shape[0])
    factors = jnp.where(
        (order < here)[:, None], jnp.exp(jnp.minimum(before_here[None, :] - running, 0.0)), 0.0
    )
    prefix = jnp.einsum(
        "nh,nhab->hab",
        factors,
        lax.all_gather(block_state[None], "tm", axis=0, tiled=True),
        precision=highest,
    )
    end_scale = jnp.exp(stretch_end).T
    carried = jnp.einsum("iha,hab->ihb", query_pos.astype(jnp.float32), prefix, precision=highest)
    mixed = local_out + end_scale[:, :, None] * carried
    inv_rms = lax.rsqrt(jnp.mean(mixed * mixed, axis=2) + EPSILON)
    gain_heads = norm_gain.reshape(heads, head_size)
    attended = (
        (mixed * inv_rms[:, :, None] * gain_heads)
        .astype(jnp.bfloat16)
        .reshape(tok_rows, heads * head_size)
    )
    layer_out = lax.psum_scatter(
        jnp.dot(attended, out_weight, preferred_element_type=jnp.float32).astype(jnp.bfloat16),
        "tensor",
        scatter_dimension=0,
        tiled=True,
    )
    out_grad = lax.dot_general(
        lax.all_gather(out_cotangent, "tensor", axis=0, tiled=True),
        out_weight,
        (((1,), (1,)), ((), ())),
        preferred_element_type=jnp.float32,
    ).reshape(tok_rows, heads, head_size)
    gained = out_grad * gain_heads
    along = jnp.mean(mixed * gained, axis=2)
    cube = inv_rms * inv_rms * inv_rms
    mixed_grad = (inv_rms[:, :, None] * gained - mixed * (cube * along)[:, :, None]).astype(
        jnp.bfloat16
    )
    prob_grad = jnp.einsum(
        "ihb,jhb->hij", mixed_grad, value_act, preferred_element_type=jnp.float32
    )
    score_grad = (weights * prob_grad).astype(jnp.bfloat16)
    value_local = jnp.einsum("hij,ihb->jhb", probs, mixed_grad, preferred_element_type=jnp.float32)
    query_local = jnp.einsum(
        "hij,jha->iha", score_grad, key_pos, preferred_element_type=jnp.float32
    )
    key_local = jnp.einsum(
        "hij,iha->jha", score_grad, query_pos, preferred_element_type=jnp.float32
    )
    scaled_query = (end_scale[:, :, None] * query_pos).astype(jnp.bfloat16)
    state_grad = jnp.einsum(
        "iha,ihb->hab", scaled_query, mixed_grad, preferred_element_type=jnp.float32
    )
    later_decay, later = entering((block_decay, state_grad), "tm", chain_combine, identity)
    value_carry = jnp.einsum("jha,hab->jhb", decayed.astype(jnp.float32), later, precision=highest)
    key_carry = key_scale[:, :, None] * jnp.einsum(
        "jhb,hab->jha", value_act.astype(jnp.float32), later, precision=highest
    )
    query_carry = end_scale[:, :, None] * jnp.einsum(
        "ihb,hab->iha", mixed_grad.astype(jnp.float32), prefix, precision=highest
    )
    flat = (tok_rows, heads * head_size)
    query_grad = (
        jnp.where(
            query_input.reshape(tok_rows, heads, head_size) > 0, query_local + query_carry, 0.0
        )
        .astype(jnp.bfloat16)
        .reshape(flat)
    )
    key_grad = (
        jnp.where(key_input.reshape(tok_rows, heads, head_size) > 0, key_local + key_carry, 0.0)
        .astype(jnp.bfloat16)
        .reshape(flat)
    )
    value_grad = (value_local + value_carry).astype(jnp.bfloat16).reshape(flat)
    return (layer_out, query_grad, key_grad, value_grad)


def solution(mesh):
    return jax.shard_map(
        on_device,
        mesh=mesh,
        in_specs=(
            P("tm", "tensor"),
            P("tm", "tensor"),
            P("tm", "tensor"),
            P("tensor", "tm"),
            P("tm"),
            P("tensor"),
            P("tensor", None),
            P(("tm", "tensor"), None),
        ),
        out_specs=(
            P(("tm", "tensor"), None),
            P("tm", "tensor"),
            P("tm", "tensor"),
            P("tm", "tensor"),
        ),
        check_vma=False,
    )
```

profile of v0, /device:TPU:4, one launch (start us, length us, event | category | flops | bytes accessed | tf_op | source)
XLA Modules:
  0.0 452.0 jit_solution(3236923922282822395)
XLA Ops:
  11.1 1.8 fusion.19
  13.0 1.3 dynamic-slice
  15.3 150.5 %all-reduce.2 = (f32[128]{0:T(128)S(1)}, f32[128]{0:T(128)S(1)}) all-reduce(f32[128]{0:T(128)S(1)} %dynamic-update-slice, f32[128]{0:T(128)S(1)} %dynamic-update-slice.1), channel_id=2, replica_groups=mesh['tm'=64,'tensor'=8] {'tm'}, use_global_device_ids=true, to_apply=%add | all-reduce | flops 256 | bytes 2048
  167.9 1.1 convolution_bitcast_fusion.5
  169.1 4.0 fusion.27
  173.1 36.5 %all-gather.10.cloned.1.call-done = f32[128,128,128]{2,1,0:T(8,128)} async-done(((f32[2,128,128]{2,1,0:T(8,128)}), f32[128,128,128]{2,1,0:T(8,128)}) %all-gather.10.cloned.1.call-update) | async-done | bytes 8388624 | tf_op jit(solution)/shard_map/all_gather | solution.py:75
  209.7 12.4 %fusion = f32[2,1,128,128]{3,1,2,0:T(1,128)S(1)} fusion(f32[64,2,1,1]{0,2,3,1:T(1,128)S(1)} %copy.95, f32[64,2,128,128]{3,2,1,0:T(8,128)} %bitcast.118), kind=kOutput, calls=%fused_computation.2 | convolution fusion | flops 25165824 | bytes 8520192 | tf_op jit(solution)/shard_map/nh,nhab->hab/dot_general | solution.py:72
  224.6 3.7 convolution_convert_fusion
  230.8 1.6 fusion.3
  233.5 1.0 fusion.13
  234.5 1.7 copy.90
  236.3 1.0 fusion.28
  237.3 1.4 convolution_bitcast_fusion.1
  238.7 137.0 %all-gather.12.cloned.1.call-done = f32[128,128,128]{2,1,0:T(8,128)} async-done(((f32[2,128,128]{2,1,0:T(8,128)}), f32[128,128,128]{2,1,0:T(8,128)}) %all-gather.12.cloned.1.call-update) | async-done | bytes 8388624 | tf_op jit(solution)/shard_map/all_gather | solution.py:13
  375.7 65.7 %while.14 = (s32[]{:T(128)}, f32[2,128,128]{2,1,0:T(8,128)S(1)}, s32[]{:T(128)}, f32[64,2]{1,0:T(8,128)S(1)}, f32[64,2,128,128]{3,2,1,0:T(8,128)}, /*index=5*/s32[]{:T(128)}, s32[]{:T(128)}, s32[]{:T(128)}, s32[]{:T(128)}) while((s32[]{:T(128)}, f32[2,128,128]{2,1,0:T(8,128)S(1)}, s32[]{:T(128)}, f32[64,2]{1,0:T(8,128)S(1)}, ...), condition=%wide.region_8.9_spmd, body=%wide.region_7.8_spmd.sunk | while | flops 65542 | bytes 393387 | solution.py:22
  375.8 1.0 bitcast_add_fusion.2
  376.8 1.0 bitcast_add_fusion.2
  377.8 1.0 bitcast_add_fusion.2
  383.0 1.0 bitcast_add_fusion.2
  384.1 1.0 bitcast_add_fusion.2
  385.1 1.0 bitcast_add_fusion.2
  386.2 1.0 bitcast_add_fusion.2
  387.2 1.0 bitcast_add_fusion.2
  388.2 1.0 bitcast_add_fusion.2
  389.3 1.0 bitcast_add_fusion.2
  390.3 1.0 bitcast_add_fusion.2
  391.4 1.0 bitcast_add_fusion.2
  392.4 1.0 bitcast_add_fusion.2
  393.5 1.0 bitcast_add_fusion.2
  394.5 1.0 bitcast_add_fusion.2
  395.6 1.0 bitcast_add_fusion.2
  396.6 1.0 bitcast_add_fusion.2
  397.6 1.0 bitcast_add_fusion.2
  398.7 1.0 bitcast_add_fusion.2
  399.7 1.0 bitcast_add_fusion.2
  400.8 1.0 bitcast_add_fusion.2
  401.8 1.0 bitcast_add_fusion.2
  402.9 1.0 bitcast_add_fusion.2
  403.9 1.0 bitcast_add_fusion.2
  405.0 1.0 bitcast_add_fusion.2
  406.0 1.0 bitcast_add_fusion.2
  407.1 1.0 bitcast_add_fusion.2
  408.1 1.0 bitcast_add_fusion.2
  409.1 1.0 bitcast_add_fusion.2
  410.2 1.0 bitcast_add_fusion.2
  411.2 1.0 bitcast_add_fusion.2
  412.3 1.0 bitcast_add_fusion.2
  413.3 1.0 bitcast_add_fusion.2
  418.5 1.0 bitcast_add_fusion.2
  419.6 1.0 bitcast_add_fusion.2
  420.6 1.0 bitcast_add_fusion.2
  421.7 1.0 bitcast_add_fusion.2
  422.7 1.0 bitcast_add_fusion.2
  423.7 1.0 bitcast_add_fusion.2
  424.8 1.0 bitcast_add_fusion.2
  425.8 1.0 bitcast_add_fusion.2
  426.9 1.0 bitcast_add_fusion.2
  427.9 1.0 bitcast_add_fusion.2
  428.9 1.0 bitcast_add_fusion.2
  430.0 1.0 bitcast_add_fusion.2
  431.0 1.0 bitcast_add_fusion.2
  432.1 1.0 bitcast_add_fusion.2
  441.4 1.0 fusion.14
  442.5 1.7 copy.92
  (150 shorter events, 30.2 us)
Async XLA Ops:
  7.2 161.9 %copy-start = (bf16[256,4096]{1,0:T(8,128)(2,1)S(1)}, bf16[256,4096]{1,0:T(8,128)(2,1)}, u32[]{:S(2)}) copy-start(bf16[256,4096]{1,0:T(8,128)(2,1)} %param.16) | copy-start | bytes 6291460
  7.2 159.1 %copy-start.7 = (bf16[384,256]{1,0:T(8,128)(2,1)S(1)}, bf16[384,256]{1,0:T(8,128)(2,1)}, u32[]{:S(2)}) copy-start(bf16[384,256]{1,0:T(8,128)(2,1)} %param.10) | copy-start | bytes 589828
  7.2 159.3 %copy-start.9 = (s32[384]{0:T(512)S(1)}, s32[384]{0:T(512)}, u32[]{:S(2)}) copy-start(s32[384]{0:T(512)} %param.14) | copy-start | bytes 4612
  7.2 161.9 %all-gather.8.cloned.1.call-start = ((), (), s32[]{:S(2)}) async-start(), calls=%async_computation.2 | async-start | bytes 3538944 | tf_op jit(solution)/shard_map/all_gather | solution.py:95
  7.9 201.7 %all-gather.10.cloned.1.call-start = ((), (), s32[]{:S(2)}) async-start(), calls=%async_computation.3 | async-start | bytes 8519680 | tf_op jit(solution)/shard_map/all_gather | solution.py:75
  12.9 155.1 %copy-start.5 = (bf16[384,256]{1,0:T(8,128)(2,1)S(1)}, bf16[384,256]{1,0:T(8,128)(2,1)}, u32[]{:S(2)}) copy-start(bf16[384,256]{1,0:T(8,128)(2,1)} %param.12) | copy-start | bytes 589828
  12.9 362.8 %all-gather.12.cloned.1.call-start = ((), (), s32[]{:S(2)}) async-start(), calls=%async_computation.4 | async-start | bytes 8519680 | tf_op jit(solution)/shard_map/all_gather | solution.py:13
  166.7 0.7 copy-start.8
  209.7 12.5 %copy-start.3 = (f32[384,256]{0,1:T(8,128)S(1)}, f32[384,256]{0,1:T(8,128)}, u32[]{:S(2)}) copy-start(f32[384,256]{0,1:T(8,128)} %fusion.27) | copy-start | bytes 1179652
  209.7 12.5 %copy-start.4 = (f32[384,2,128]{0,2,1:T(8,128)S(1)}, f32[384,2,128]{0,2,1:T(8,128)}, u32[]{:S(2)}) copy-start(f32[384,2,128]{0,2,1:T(8,128)} %convolution_bitcast_fusion.5) | copy-start | bytes 1179652
  209.7 12.5 %copy-start.10 = (f32[256]{0:T(256)S(1)}, f32[256]{0:T(256)}, u32[]{:S(2)}) copy-start(f32[256]{0:T(256)} %param.15) | copy-start | bytes 3076
  224.4 221.1 %reduce-scatter.2.cloned.1.call-start = ((), (), s32[]{:S(2)}) async-start(), calls=%async_computation.1 | async-start | bytes 3538944 | tf_op jit(solution)/shard_map/reduce_scatter | solution.py:88
  232.4 0.8 copy-start.1
  237.3 204.1 %copy-start.2 = (f32[2,128,384]{2,1,0:T(8,128)S(1)}, f32[2,128,384]{2,1,0:T(8,128)}, u32[]{:S(2)}) copy-start(f32[2,128,384]{2,1,0:T(8,128)} %fusion.28) | copy-start | bytes 1179652
  238.7 205.5 %copy-start.6 = (bf16[384,256]{1,0:T(8,128)(2,1)S(1)}, bf16[384,256]{1,0:T(8,128)(2,1)}, u32[]{:S(2)}) copy-start(bf16[384,256]{1,0:T(8,128)(2,1)} %param.12) | copy-start | bytes 589828
Sparse Core Ops, SparseCore 0:
  10.1 38.4 all-gather.7
  52.1 157.4 all-gather.9
  224.5 151.1 all-gather.11
  379.0 33.6 reduce-scatter.1
where the time goes:
time: 454 us; the launch traced here: 452 us
  waiting for transfers between devices  174 us (38%)
  blocking collectives  151 us (33%)
  other arithmetic  68.2 us (15%)
  matrix products  31.7 us (7%)
  between operations  14.7 us (3%)
  local copies, waits for them, and re-layouts  9.98 us (2%)
    unnamed x1, blocking collectives  151 us
    all_gather x1, waiting for transfers between devices, entering(): gathered = jax.tree.map(lambda a: lax.all_gather(a, axis), part)  137 us
    add x63, other arithmetic, chain_combine(): later[0][:, None, None] * earlier[1] + later[1]  62.8 us
    all_gather x1, waiting for transfers between devices, on_device(): lax.all_gather(block_state[None], 'tm', axis=0, tiled=True)  36.5 us
    dot_general x1, matrix products, on_device(): jnp.einsum('nh,nhab->hab', factors, lax.all_gather(block_state[None], 'tm...  12.4 us
  transfers between devices with their start and end apart: 4, of which 2 were waited for; matrix products, arithmetic and copies ran while one was open for 21% of the time, Pallas kernels for 0%

commit v1 on v0

--- a/solution.py
+++ b/solution.py
@@ -1,29 +1,69 @@
 import jax
 import jax.numpy as jnp
 from jax import lax
+from jax.experimental import pallas as pl
+from jax.experimental.pallas import tpu as pltpu
 from jax.sharding import PartitionSpec as P
 
 EPSILON = 1e-06
 
 
-def entering(part, axis, combine, identity):
-    count = lax.axis_size(axis)
-    place = lax.axis_index(axis)
-    ahead = count - 1 - place
-    gathered = jax.tree.map(lambda a: lax.all_gather(a, axis), part)
-    state = jax.tree.map(lambda a, e: jnp.zeros_like(a) + jnp.asarray(e, a.dtype), part, identity)
-
-    def one(turn, state):
-        source = count - 1 - turn
-        return combine(
-            state, jax.tree.map(lambda a: lax.dynamic_index_in_dim(a, source, 0, False), gathered)
-        )
-
-    return lax.fori_loop(0, ahead, one, state)
+def forward_scan_kernel(got_ref, out_ref, gate_ref):
+    count = got_ref.shape[0]
+    rows = out_ref.shape[1]
+    got = got_ref[...].astype(jnp.float32)
+    decay = got[:, rows : rows + 1, :] + got[:, rows + 1 : rows + 2, :] + got[:, rows + 2 : rows + 3, :]
+    gate = jnp.exp(decay)
+    gate_ref[...] = jnp.broadcast_to(gate, gate_ref.shape)
+    state = jnp.zeros(out_ref.shape[1:], jnp.float32)
+    for block in range(count):
+        out_ref[block] = state.astype(out_ref.dtype)
+        state = gate[block] * state + got[block, :rows, :]
 
 
-def chain_combine(earlier, later):
-    return (earlier[0] * later[0], later[0][:, None, None] * earlier[1] + later[1])
+def reverse_scan_kernel(got_ref, gate_ref, out_ref):
+    count = got_ref.shape[0]
+    state = jnp.zeros(out_ref.shape[1:], jnp.float32)
+    for block in range(count - 1, -1, -1):
+        out_ref[block] = state.astype(out_ref.dtype)
+        state = gate_ref[block] * state + got_ref[block].astype(jnp.float32)
+
+
+def exchange(pieces):
+    return lax.all_to_all(pieces, "tm", 0, 0, tiled=True)
+
+
+def entering_forward(block_state, block_end, count):
+    heads, size, width = block_state.shape
+    rows = heads * size // count
+    pieces = block_state.reshape(count, rows, width).astype(jnp.bfloat16)
+    high = block_end.astype(jnp.bfloat16)
+    rest = block_end - high.astype(jnp.float32)
+    middle = rest.astype(jnp.bfloat16)
+    low = (rest - middle.astype(jnp.float32)).astype(jnp.bfloat16)
+    parts = jnp.stack([high, middle, low, jnp.zeros_like(low)], axis=1)
+    parts = jnp.repeat(parts, count // heads, axis=0)
+    tail = jnp.broadcast_to(parts[:, :, None], (count, 4, width))
+    got = exchange(jnp.concatenate([pieces, tail], axis=1))
+    mine, gate = pl.pallas_call(
+        forward_scan_kernel,
+        out_shape=(
+            jax.ShapeDtypeStruct((count, rows, width), jnp.bfloat16),
+            jax.ShapeDtypeStruct((count, rows, width), jnp.float32),
+        ),
+    )(got)
+    return exchange(mine).reshape(heads, size, width), gate
+
+
+def entering_reverse(state_grad, gate, count):
+    heads, size, width = state_grad.shape
+    rows = heads * size // count
+    got = exchange(state_grad.reshape(count, rows, width).astype(jnp.bfloat16))
+    mine = pl.pallas_call(
+        reverse_scan_kernel,
+        out_shape=jax.ShapeDtypeStruct((count, rows, width), jnp.bfloat16),
+    )(got, gate)
+    return exchange(mine).reshape(heads, size, width)
 
 
 def on_device(
@@ -36,7 +76,6 @@
     out_weight,
     out_cotangent,
 ):
-    highest = lax.Precision.HIGHEST
     tok_rows = query_input.shape[0]
     heads = log_decay.shape[0]
     head_size = query_input.shape[1] // heads
@@ -59,24 +98,9 @@
     key_scale = jnp.exp(block_end[:, None] - cumulative).T
     decayed = (key_scale[:, :, None] * key_pos).astype(jnp.bfloat16)
     block_state = jnp.einsum("jha,jhb->hab", decayed, value_act, preferred_element_type=jnp.float32)
-    block_decay = jnp.exp(block_end)
-    identity = (jnp.ones_like(block_decay), jnp.zeros_like(block_state))
-    totals = lax.all_gather(block_end[None, :], "tm", axis=0, tiled=True)
-    running = jnp.cumsum(totals, axis=0)
-    here = lax.axis_index("tm")
-    before_here = lax.dynamic_index_in_dim(running, jnp.maximum(here - 1, 0), 0, keepdims=False)
-    order = jnp.arange(totals.shape[0])
-    factors = jnp.where(
-        (order < here)[:, None], jnp.exp(jnp.minimum(before_here[None, :] - running, 0.0)), 0.0
-    )
-    prefix = jnp.einsum(
-        "nh,nhab->hab",
-        factors,
-        lax.all_gather(block_state[None], "tm", axis=0, tiled=True),
-        precision=highest,
-    )
+    prefix, gate = entering_forward(block_state, block_end, lax.axis_size("tm"))
     end_scale = jnp.exp(stretch_end).T
-    carried = jnp.einsum("iha,hab->ihb", query_pos.astype(jnp.float32), prefix, precision=highest)
+    carried = jnp.einsum("iha,hab->ihb", query_pos, prefix, preferred_element_type=jnp.float32)
     mixed = local_out + end_scale[:, :, None] * carried
     inv_rms = lax.rsqrt(jnp.mean(mixed * mixed, axis=2) + EPSILON)
     gain_heads = norm_gain.reshape(heads, head_size)
@@ -118,13 +142,13 @@
     state_grad = jnp.einsum(
         "iha,ihb->hab", scaled_query, mixed_grad, preferred_element_type=jnp.float32
     )
-    later_decay, later = entering((block_decay, state_grad), "tm", chain_combine, identity)
-    value_carry = jnp.einsum("jha,hab->jhb", decayed.astype(jnp.float32), later, precision=highest)
+    later = entering_reverse(state_grad, gate, lax.axis_size("tm"))
+    value_carry = jnp.einsum("jha,hab->jhb", decayed, later, preferred_element_type=jnp.float32)
     key_carry = key_scale[:, :, None] * jnp.einsum(
-        "jhb,hab->jha", value_act.astype(jnp.float32), later, precision=highest
+        "jhb,hab->jha", value_act, later, preferred_element_type=jnp.float32
     )
     query_carry = end_scale[:, :, None] * jnp.einsum(
-        "ihb,hab->iha", mixed_grad.astype(jnp.float32), prefix, precision=highest
+        "ihb,hab->iha", mixed_grad, prefix, preferred_element_type=jnp.float32
     )
     flat = (tok_rows, heads * head_size)
     query_grad = (

time: 454 us -> 133 us (0.29)
  the two profiles are of different devices: /device:TPU:4 before, /device:TPU:2 now
where the time goes in v1:
time: 133 us; the launch traced here: 132 us
  waiting for transfers between devices  52 us (39%)
  starting transfers between devices  34.6 us (26%)
  matrix products  16.4 us (12%)
  between operations  14.3 us (11%)
  local copies, waits for them, and re-layouts  7.09 us (5%)
  other arithmetic  4.66 us (4%)
  Pallas kernels  3.4 us (3%)
    all_to_all x4, waiting for transfers between devices, exchange(): return lax.all_to_all(pieces, 'tm', 0, 0, tiled=True)  51.2 us
    all_to_all x4, starting transfers between devices, exchange(): return lax.all_to_all(pieces, 'tm', 0, 0, tiled=True)  34.5 us
    unnamed x30, local copies, waits for them, and re-layouts  4.05 us
    dot_general x1, matrix products, on_device(): lax.dot_general(lax.all_gather(out_cotangent, 'tensor', axis=0, tiled=Tru...  3.9 us
  transfers between devices with their start and end apart: 6, of which 4 were waited for; matrix products, arithmetic and copies ran while one was open for 17% of the time, Pallas kernels for 3%

profile of v1, /device:TPU:2, one launch (start us, length us, event | category | flops | bytes accessed | tf_op | source)
XLA Modules:
  0.0 132.4 jit_solution(13014824853351649645)
XLA Ops:
  7.2 0.0 copy-start
  7.2 0.0 copy-start.4
  7.2 0.0 copy-start.11
  7.2 0.0 all-gather.2.cloned.1.call-start
  7.2 0.7 all-gather.2.cloned.1.call-update
  7.9 0.7 reshape.138
  8.6 0.6 reduce-window.6
  9.2 0.2 slice_reduce_fusion
  9.4 0.2 reduce-window.9
  9.6 0.1 add_bitcast_fusion
  9.7 1.0 broadcast_maximum_fusion
  10.7 0.2 copy.55
  10.8 0.1 pad.5.clone
  10.9 0.2 subtract_convert_fusion.1
  11.1 0.1 maximum_maximum_fusion
  11.2 0.1 exponential_bitcast_fusion
  11.2 0.2 convolution_convert_fusion.2
  11.5 0.1 broadcast_in_dim.68
  11.6 0.7 pad_maximum_fusion
  12.3 19.0 %all-to-all-start = ((bf16[64,8,128]{2,1,0:T(8,128)(2,1)}), bf16[64,8,128]{2,1,0:T(8,128)(2,1)}, u32[]{:S(2)}, u32[]{:S(2)}) async-start(bf16[64,8,128]{2,1,0:T(8,128)(2,1)} %pad_maximum_fusion), calls=%async_computation | async-start | bytes 262144 | tf_op jit(solution)/shard_map/all_to_all | solution.py:33
  31.3 0.2 broadcast_compare_fusion.1
  31.6 0.0 copy-start.9
  31.6 0.3 select_reduce_fusion
  31.9 0.2 copy.54
  32.1 0.2 copy-done.9
  32.2 0.5 fusion
  32.8 0.4 copy-done.5
  33.2 0.4 convolution_bitcast_fusion.5
  33.6 15.3 %all-to-all-done.got_ref = bf16[64,8,128]{2,1,0:T(8,128)(2,1)} async-done(((bf16[64,8,128]{2,1,0:T(8,128)(2,1)}), bf16[64,8,128]{2,1,0:T(8,128)(2,1)}, u32[]{:S(2)}, u32[]{:S(2)}) %all-to-all-start) | async-done | bytes 131104 | tf_op jit(solution)/shard_map/all_to_all | solution.py:33
  48.9 1.7 %shard_map.111 = (bf16[64,4,128]{2,1,0:T(4,128)(2,1)}, f32[64,4,128]{2,1,0:T(4,128)}) custom-call(bf16[64,8,128]{2,1,0:T(8,128)(2,1)} %all-to-all-done.got_ref), custom_call_target="tpu_custom_call" | custom-call | tf_op jit(solution)/shard_map/pallas_call | solution.py:48
  50.5 4.6 %all-to-all-start.1 = ((bf16[64,4,128]{2,1,0:T(4,128)(2,1)}), bf16[64,4,128]{2,1,0:T(4,128)(2,1)S(1)}, u32[]{:S(2)}, u32[]{:S(2)}) async-start(bf16[64,4,128]{2,1,0:T(4,128)(2,1)} %get-tuple-element.6), calls=%async_computation.1 | async-start | bytes 131072 | tf_op jit(solution)/shard_map/all_to_all | solution.py:33
  55.2 0.0 reduce-scatter.2.cloned.1.call-start
  55.2 0.0 all-gather.2.cloned.1.call-done
  55.2 3.9 %fusion.25 = f32[384,256]{0,1:T(8,128)} fusion(bf16[384,4096]{1,0:T(8,128)(2,1)} %all-gather.2.cloned.1.call-done, bf16[256,4096]{1,0:T(8,128)(2,1)S(1)} %copy-done), kind=kOutput, calls=%fused_computation.63 | convolution fusion | flops 805306368 | bytes 5636096 | tf_op jit(solution)/shard_map/dot_general | solution.py:118
  59.2 11.3 %all-to-all-done.1 = bf16[64,4,128]{2,1,0:T(4,128)(2,1)S(1)} async-done(((bf16[64,4,128]{2,1,0:T(4,128)(2,1)}), bf16[64,4,128]{2,1,0:T(4,128)(2,1)S(1)}, u32[]{:S(2)}, u32[]{:S(2)}) %all-to-all-start.1) | async-done | bytes 65568 | tf_op jit(solution)/shard_map/all_to_all | solution.py:33
  70.5 1.4 %multiply_reduce_fusion = (f32[384,2]{0,1:T(2,128)S(1)}, f32[384,2]{0,1:T(2,128)S(1)}, f32[384,2,128]{0,2,1:T(8,128)S(1)}) fusion(f32[384,256]{0,1:T(8,128)} %fusion.25, f32[2,128]{1,0:T(2,128)} %bitcast.131, f32[384,2,128]{0,2,1:T(8,128)S(1)} %convolution_bitcast_fusion.5, bf16[2,128,128]{2,1,0:T(8,128)(2,1)S(1)} %bitcast.119, ...), kind=kOutput, calls=%fused_computation.29 | convolution fusion | flops 25852416 | bytes 1452032 | tf_op jit(solution)/shard_map/iha,hab->ihb/dot_general | solution.py:103
  71.8 0.0 copy-done.1
  71.9 0.0 copy-done.12
  71.9 0.2 subtract_convert_fusion
  72.0 2.7 %convolution_convert_fusion = bf16[384,4096]{1,0:T(8,128)(2,1)} fusion(bf16[384,256]{0,1:T(8,128)(2,1)S(1)} %bitcast.118, bf16[256,4096]{1,0:T(8,128)(2,1)S(1)} %copy-done), kind=kOutput, calls=%fused_computation | convolution fusion | flops 806879232 | bytes 5439488 | tf_op jit(solution)/shard_map/dot_general | solution.py:113
  74.7 0.0 reduce-scatter.2.cloned.1.call-update
  74.7 0.9 copy-done.3
  75.6 0.1 broadcast_compare_fusion.3
  75.7 0.8 copy.62
  76.5 1.0 broadcast_compare_fusion.2
  77.5 0.8 copy.66
  78.3 0.8 convolution_convert_fusion.1
  79.2 5.4 %all-to-all-start.2 = ((bf16[64,4,128]{2,1,0:T(4,128)(2,1)}), bf16[64,4,128]{2,1,0:T(4,128)(2,1)}, u32[]{:S(2)}, u32[]{:S(2)}) async-start(bf16[64,4,128]{2,1,0:T(4,128)(2,1)} %bitcast.123), calls=%async_computation.3 | async-start | bytes 131072 | tf_op jit(solution)/shard_map/all_to_all | solution.py:33
  84.6 0.0 copy-start.10
  84.6 1.0 fusion.26
  85.7 0.5 fusion.1
  86.2 1.1 convolution_bitcast_fusion.3
  87.3 12.2 %all-to-all-done.2.got_ref = bf16[64,4,128]{2,1,0:T(4,128)(2,1)} async-done(((bf16[64,4,128]{2,1,0:T(4,128)(2,1)}), bf16[64,4,128]{2,1,0:T(4,128)(2,1)}, u32[]{:S(2)}, u32[]{:S(2)}) %all-to-all-start.2) | async-done | bytes 65568 | tf_op jit(solution)/shard_map/all_to_all | solution.py:33
  99.5 1.7 %shard_map.112 = bf16[64,4,128]{2,1,0:T(4,128)(2,1)} custom-call(bf16[64,4,128]{2,1,0:T(4,128)(2,1)} %all-to-all-done.2.got_ref, f32[64,4,128]{2,1,0:T(4,128)} %get-tuple-element.7.gate_ref), custom_call_target="tpu_custom_call" | custom-call | tf_op jit(solution)/shard_map/pallas_call | solution.py:62
  101.2 5.4 %all-to-all-start.3 = ((bf16[64,4,128]{2,1,0:T(4,128)(2,1)}), bf16[64,4,128]{2,1,0:T(4,128)(2,1)}, u32[]{:S(2)}, u32[]{:S(2)}) async-start(bf16[64,4,128]{2,1,0:T(4,128)(2,1)} %shard_map.112), calls=%async_computation.4 | async-start | bytes 131072 | tf_op jit(solution)/shard_map/all_to_all | solution.py:33
  106.7 1.3 fusion.11
  107.9 0.8 copy.71
  108.8 0.3 convolution_bitcast_fusion.1
  109.0 0.0 copy-start.7
  109.1 12.5 %all-to-all-done.3 = bf16[64,4,128]{2,1,0:T(4,128)(2,1)} async-done(((bf16[64,4,128]{2,1,0:T(4,128)(2,1)}), bf16[64,4,128]{2,1,0:T(4,128)(2,1)}, u32[]{:S(2)}, u32[]{:S(2)}) %all-to-all-start.3) | async-done | bytes 65568 | tf_op jit(solution)/shard_map/all_to_all | solution.py:33
  121.5 1.3 fusion.12
  122.8 0.8 copy.73
  123.7 1.1 fusion.10
  124.7 0.8 copy.72
  (21 shorter events, 0.1 us)
Async XLA Ops:
  7.2 48.1 %copy-start = (bf16[256,4096]{1,0:T(8,128)(2,1)S(1)}, bf16[256,4096]{1,0:T(8,128)(2,1)}, u32[]{:S(2)}) copy-start(bf16[256,4096]{1,0:T(8,128)(2,1)} %param.14) | copy-start | bytes 6291460
  7.2 4.1 %copy-start.4 = (bf16[384,256]{1,0:T(8,128)(2,1)S(1)}, bf16[384,256]{1,0:T(8,128)(2,1)}, u32[]{:S(2)}) copy-start(bf16[384,256]{1,0:T(8,128)(2,1)} %param.10) | copy-start | bytes 589828
  7.2 24.1 %copy-start.11 = (s32[384]{0:T(512)S(1)}, s32[384]{0:T(512)}, u32[]{:S(2)}) copy-start(s32[384]{0:T(512)} %param.12) | copy-start | bytes 4612
  7.2 48.0 %all-gather.2.cloned.1.call-start = ((), (), s32[]{:S(2)}) async-start(), calls=%async_computation.6 | async-start | bytes 3538944 | tf_op jit(solution)/shard_map/all_gather | solution.py:119
  9.7 22.2 %copy-start.2 = (bf16[384,256]{1,0:T(8,128)(2,1)S(1)}, bf16[384,256]{1,0:T(8,128)(2,1)}, u32[]{:S(2)}) copy-start(bf16[384,256]{1,0:T(8,128)(2,1)} %param.8) | copy-start | bytes 589828
  12.3 36.5 %all-to-all-start = ((bf16[64,8,128]{2,1,0:T(8,128)(2,1)}), bf16[64,8,128]{2,1,0:T(8,128)(2,1)}, u32[]{:S(2)}, u32[]{:S(2)}) async-start(bf16[64,8,128]{2,1,0:T(8,128)(2,1)} %pad_maximum_fusion), calls=%async_computation | async-start | bytes 262144 | tf_op jit(solution)/shard_map/all_to_all | solution.py:33
  31.6 0.7 copy-start.9
  32.2 1.0 copy-start.5
  50.5 19.9 %all-to-all-start.1 = ((bf16[64,4,128]{2,1,0:T(4,128)(2,1)}), bf16[64,4,128]{2,1,0:T(4,128)(2,1)S(1)}, u32[]{:S(2)}, u32[]{:S(2)}) async-start(bf16[64,4,128]{2,1,0:T(4,128)(2,1)} %get-tuple-element.6), calls=%async_computation.1 | async-start | bytes 131072 | tf_op jit(solution)/shard_map/all_to_all | solution.py:33
  55.2 70.4 %reduce-scatter.2.cloned.1.call-start = ((), (), s32[]{:S(2)}) async-start(), calls=%async_computation.5 | async-start | bytes 3538944 | tf_op jit(solution)/shard_map/reduce_scatter | solution.py:112
  70.5 1.4 %copy-start.1 = (f32[384,256]{0,1:T(8,128)S(1)}, f32[384,256]{0,1:T(8,128)}, u32[]{:S(2)}) copy-start(f32[384,256]{0,1:T(8,128)} %fusion.25) | copy-start | bytes 1179652
  70.5 1.4 %copy-start.12 = (f32[256]{0:T(256)S(1)}, f32[256]{0:T(256)}, u32[]{:S(2)}) copy-start(f32[256]{0:T(256)} %param.13) | copy-start | bytes 3076
  74.7 0.9 copy-start.3
  76.5 9.2 %copy-start.6 = (bf16[384,256]{1,0:T(8,128)(2,1)S(1)}, bf16[384,256]{1,0:T(8,128)(2,1)}, u32[]{:S(2)}) copy-start(bf16[384,256]{1,0:T(8,128)(2,1)} %param.10) | copy-start | bytes 589828
  79.2 20.3 %all-to-all-start.2 = ((bf16[64,4,128]{2,1,0:T(4,128)(2,1)}), bf16[64,4,128]{2,1,0:T(4,128)(2,1)}, u32[]{:S(2)}, u32[]{:S(2)}) async-start(bf16[64,4,128]{2,1,0:T(4,128)(2,1)} %bitcast.123), calls=%async_computation.3 | async-start | bytes 131072 | tf_op jit(solution)/shard_map/all_to_all | solution.py:33
  84.6 1.0 copy-start.10
  101.2 20.3 %all-to-all-start.3 = ((bf16[64,4,128]{2,1,0:T(4,128)(2,1)}), bf16[64,4,128]{2,1,0:T(4,128)(2,1)}, u32[]{:S(2)}, u32[]{:S(2)}) async-start(bf16[64,4,128]{2,1,0:T(4,128)(2,1)} %shard_map.112), calls=%async_computation.4 | async-start | bytes 131072 | tf_op jit(solution)/shard_map/all_to_all | solution.py:33
  109.0 14.6 %copy-start.7 = (bf16[384,256]{1,0:T(8,128)(2,1)S(1)}, bf16[384,256]{1,0:T(8,128)(2,1)}, u32[]{:S(2)}) copy-start(bf16[384,256]{1,0:T(8,128)(2,1)} %param.10) | copy-start | bytes 589828
  109.1 14.6 %copy-start.8 = (pred[384,256]{0,1:T(32,128)(4,1)S(1)}, pred[384,256]{0,1:T(32,128)(4,1)}, u32[]{:S(2)}) copy-start(pred[384,256]{0,1:T(32,128)(4,1)} %copy.66) | copy-start | bytes 294916
Sparse Core Ops, SparseCore 0:
  10.1 38.8 all-gather.1
  74.8 30.3 reduce-scatter.1
